TPU v7x, 1024 devices: a whole 4x8x16 slice. The times are simulated.
1024 devices in a mesh: gx: 32 (over z, core), gy: 32 (over x, y).
Axes of the slice: x: 4, y: 8, z: 16, core: 2. Of those that a mesh axis runs over, the one named last changes fastest.
Arguments:
- density: bfloat16 [128, 128, 1024], P('gx', 'gy'), may hold values from -6 to 6
- p2m_operator: bfloat16 [64, 56], replicated, may hold values from -0.75 to 0.75
- m2l_table: bfloat16 [7, 7, 7, 56, 56], replicated, may hold values from -0.0625 to 0.0625
- near_table: bfloat16 [3, 3, 3, 64, 64], replicated, may hold values from -0.15625 to 0.15625
- l2p_operator: bfloat16 [56, 64], replicated, may hold values from -0.75 to 0.75
Outputs:
- potential: float32 [128, 128, 1024], P('gx', 'gy')
All inputs are finite; a program needn't handle non-finite values.
Results may differ from a plain program's by a relative error of at most 0.003.
Values may be sent and summed in bfloat16 or wider, within the bound.
A program may use at most 128 MiB of HBM per device.

v0:
```python
import jax
import jax.numpy as jnp
from jax import lax
from jax.experimental import pallas as pl
from jax.experimental.pallas import tpu as pltpu
from jax.sharding import PartitionSpec as P

BF = jnp.bfloat16
F32 = jnp.float32
MESH = pl.DeviceIdType.MESH
HALO = 2
SIDES = [(dx, dy) for dx in (-1, 0, 1) for dy in (-1, 0, 1) if (dx, dy) != (0, 0)]
SOURCE = {-1: slice(0, 2), 0: slice(0, 4), 1: slice(2, 4)}
TARGET = {-1: slice(6, 8), 0: slice(2, 6), 1: slice(0, 2)}
BLOCKS = (1, 2, 5, 6, 3, 4)


def dot(a, b):
    return jnp.dot(a, b, preferred_element_type=F32)


def left(block):
    rows, lanes = block.shape
    block = jnp.concatenate([block, jnp.zeros((rows, 128 - lanes), BF)], axis=1)
    if rows < 64:
        block = jnp.concatenate([block, jnp.zeros((64 - rows, 128), BF)], axis=0)
    return block


def swap(block):
    return pltpu.roll(block, 64, 1)


def kernel(
    density, p2m_t, m2l, near, l2p, out,
    raw, cells, table, near_raw, p2m_raw, l2p_raw,
    weights, near_weights, far0, far1, far2, near0, near1,
    in_sems, table_sems, send_sems, recv_sems,
):
    gx, gy = lax.axis_index("gx"), lax.axis_index("gy")
    nx, ny = lax.axis_size("gx"), lax.axis_size("gy")

    def present(dx, dy):
        ok = None
        for d, g, n in ((dx, gx, nx), (dy, gy, ny)):
            if d:
                test = (g + d >= 0) & (g + d < n)
                ok = test if ok is None else ok & test
        return ok

    copies_in = [
        pltpu.make_async_copy(density, raw, in_sems.at[0]),
        pltpu.make_async_copy(near, near_raw, in_sems.at[1]),
        pltpu.make_async_copy(p2m_t, p2m_raw, in_sems.at[2]),
        pltpu.make_async_copy(l2p, l2p_raw, in_sems.at[3]),
    ]
    copies_in[0].start()
    barrier = pltpu.get_barrier_semaphore()
    count = jnp.int32(0)
    for dx, dy in SIDES:
        ok = present(dx, dy)
        count = count + ok.astype(jnp.int32)

        @pl.when(ok)
        def _():
            pl.semaphore_signal(
                barrier, inc=1, device_id=(gx + dx, gy + dy), device_id_type=MESH
            )
    for c in copies_in[1:]:
        c.start()
    table_copies = [
        pltpu.make_async_copy(m2l.at[i], table.at[i], table_sems.at[i]) for i in range(7)
    ]
    for c in table_copies:
        c.start()

    for dx, dy in SIDES:
        @pl.when(jnp.logical_not(present(dx, dy)))
        def _():
            ys, xs = TARGET[-dy], TARGET[-dx]
            cells[ys, xs] = jnp.zeros((ys.stop - ys.start, xs.stop - xs.start, 8, 128), BF)

    copies_in[0].wait()
    own = raw[...].astype(F32)
    for y in range(4):
        for x in range(4):
            tile = jnp.concatenate(
                [own[x, y : y + 1, 128 * z : 128 * z + 128] for z in range(8)], axis=0
            )
            cells[HALO + y, HALO + x] = tile.astype(BF)

    lane = lax.broadcasted_iota(jnp.int32, (64, 128), 1)
    low = lane < 64
    zero = jnp.zeros((64, 128), BF)
    copies_in[1].wait()

    def build_near(i, carry):
        a = near_raw[i // 3, i % 3, 0]
        b = near_raw[i // 3, i % 3, 1]
        c = near_raw[i // 3, i % 3, 2]
        a, b, c = left(a), left(b), left(c)
        near_weights[i, 0:64] = jnp.where(low, b, swap(a))
        near_weights[i, 64:128] = jnp.where(low, c, swap(b))
        near_weights[i, 128:192] = swap(c)
        near_weights[i, 192:256] = a
        return carry

    lax.fori_loop(0, 9, build_near, 0)

    copies_in[2].wait()
    copies_in[3].wait()
    p2m_block = left(p2m_raw[...])
    p2m = jnp.concatenate([p2m_block, swap(p2m_block)], axis=0)
    l2p_block = left(l2p_raw[...])
    l2p_pair = jnp.concatenate([l2p_block, swap(l2p_block)], axis=0)

    pl.semaphore_wait(barrier, count)

    def remote(k):
        dx, dy = SIDES[k]
        return pltpu.make_async_remote_copy(
            src_ref=cells.at[
                slice(HALO + SOURCE[dy].start, HALO + SOURCE[dy].stop),
                slice(HALO + SOURCE[dx].start, HALO + SOURCE[dx].stop),
            ],
            dst_ref=cells.at[TARGET[dy], TARGET[dx]],
            send_sem=send_sems.at[k],
            recv_sem=recv_sems.at[k],
            device_id=(gx + dx, gy + dy),
            device_id_type=MESH,
        )

    for k, (dx, dy) in enumerate(SIDES):
        @pl.when(present(dx, dy))
        def _():
            remote(k).start()

    for ox in range(7):
        table_copies[ox].wait()

        def build(oy, carry):
            blocks = [left(table[ox, oy, k]) for k in range(7)]
            for slot, k in enumerate(BLOCKS):
                weights[ox, oy, 64 * slot : 64 * slot + 64] = jnp.where(
                    low, blocks[k], swap(blocks[k - 1])
                )
            return carry

        lax.fori_loop(0, 7, build, 0)
        if 2 <= ox <= 4:
            def build_close(oy, carry):
                weights[ox, oy, 64:128] = swap(left(table[ox, oy, 1]))
                weights[ox, oy, 128:192] = left(table[ox, oy, 5])
                return carry

            lax.fori_loop(2, 5, build_close, 0)

    for k, (dx, dy) in enumerate(SIDES):
        @pl.when(present(-dx, -dy))
        def _():
            remote(k).wait_recv()

    row = lax.broadcasted_iota(jnp.int32, (8, 8, 128), 1)
    half = lax.broadcasted_iota(jnp.int32, (8, 8, 128), 2) < 64

    def below(v):
        return jnp.where(row == 0, 0.0, pltpu.roll(v, 1, 1))

    def above(v):
        return jnp.where(row == 7, 0.0, pltpu.roll(v, 7, 1))

    def spread(y, carry):
        raw_rows = cells[y]
        rows = raw_rows.astype(F32)
        packed = rows.reshape(64, 128).astype(BF)
        m = lax.dot_general(
            packed, p2m, (((1,), (1,)), ((), ())), preferred_element_type=F32
        ).reshape(8, 8, 128)
        for part, v in enumerate((below(m), above(m), m)):
            ln = slice(128 * part, 128 * part + 128)
            far0[y, :, ln] = v.reshape(64, 128).astype(BF)
            far1[y, :, ln] = v[1:7].reshape(48, 128).astype(BF)
            far2[y, 0:16, ln] = jnp.concatenate([v[0], v[2]], axis=0).astype(BF)
            far2[y, 16:32, ln] = jnp.concatenate([v[5], v[7]], axis=0).astype(BF)
        edge = jnp.where(half, above(rows), below(rows))
        for part, v in enumerate((rows, edge)):
            ln = slice(128 * part, 128 * part + 128)
            near0[y, :, ln] = v.reshape(64, 128).astype(BF)
            near1[y, :, ln] = v[1:7].reshape(48, 128).astype(BF)
        return carry

    lax.fori_loop(0, 8, spread, 0)

    def sources(even, odd, x0, y0, count, lanes):
        if x0 % 2 == 0:
            ref, start = even, 8 * x0
        else:
            ref, start = odd, 8 * (x0 - 1)
        return ref[y0 : y0 + count, start : start + 32, 0:lanes].reshape(32 * count, lanes)

    close = jnp.zeros((128, 128), F32)
    for dx in range(3):
        for dy in range(3):
            close += dot(
                sources(near0, near1, 1 + dx, 1 + dy, 4, 256), near_weights[3 * dx + dy]
            )

    total = jnp.zeros((128, 128), F32)
    for ox in range(1, 6):
        for oy in range(1, 6):
            lanes = 256 if 2 <= ox <= 4 and 2 <= oy <= 4 else 384
            total += dot(
                sources(far0, far1, ox - 1, oy - 1, 4, lanes), weights[ox, oy, 0:lanes]
            )
    total = [[total[32 * y + 8 * x : 32 * y + 8 * x + 8] for x in range(4)] for y in range(4)]

    def add(value, ys, xs):
        i = 0
        for y in ys:
            for x in xs:
                total[y][x] = total[y][x] + value[8 * i : 8 * i + 8]
                i += 1

    for oy, ys, places in ((0, (1, 3), (0, 2)), (6, (0, 2), (5, 7))):
        acc = jnp.zeros((64, 128), F32)
        for ox in range(1, 6):
            lhs = jnp.concatenate(
                [sources(far0, far1, ox - 1, place, 1, 384) for place in places], axis=0
            )
            acc += dot(lhs, weights[ox, oy])
        add(acc, ys, range(4))
    for ox, xs, group in ((0, (1, 3), 0), (6, (0, 2), 1)):
        acc = jnp.zeros((64, 128), F32)
        for oy in range(1, 6):
            lhs = far2[oy - 1 : oy + 3, 16 * group : 16 * group + 16].reshape(64, 384)
            acc += dot(lhs, weights[ox, oy])
        add(acc, range(4), xs)
        for oy, ys, places in ((0, (1, 3), (0, 2)), (6, (0, 2), (5, 7))):
            lhs = jnp.concatenate(
                [far2[place, 16 * group : 16 * group + 16] for place in places], axis=0
            )
            add(dot(lhs, weights[ox, oy]), ys, xs)

    expansion = jnp.concatenate([total[y][x] for y in range(4) for x in range(4)], axis=0)
    result = close + dot(expansion.astype(BF), l2p_pair)
    for y in range(4):
        for x in range(4):
            for z in range(8):
                r = 32 * y + 8 * x + z
                out[x, y : y + 1, 128 * z : 128 * z + 128] = result[r : r + 1]

    for k, (dx, dy) in enumerate(SIDES):
        @pl.when(present(dx, dy))
        def _():
            remote(k).wait_send()


def local(density, p2m_operator, m2l_table, near_table, l2p_operator):
    anywhere = pl.BlockSpec(memory_space=pltpu.HBM)
    operands = [
        pltpu.with_memory_space_constraint(v, pltpu.HBM)
        for v in (density, p2m_operator.T, m2l_table, near_table, l2p_operator)
    ]
    return pl.pallas_call(
        kernel,
        out_shape=jax.ShapeDtypeStruct(density.shape, F32),
        in_specs=[anywhere] * 5,
        out_specs=pl.BlockSpec(memory_space=pltpu.VMEM),
        scratch_shapes=[
            pltpu.VMEM((4, 4, 1024), BF),
            pltpu.VMEM((8, 8, 8, 128), BF),
            pltpu.VMEM((7, 7, 7, 56, 56), BF),
            pltpu.VMEM((3, 3, 3, 64, 64), BF),
            pltpu.VMEM((56, 64), BF),
            pltpu.VMEM((56, 64), BF),
            pltpu.VMEM((7, 7, 384, 128), BF),
            pltpu.VMEM((9, 256, 128), BF),
            pltpu.VMEM((8, 64, 384), BF),
            pltpu.VMEM((8, 48, 384), BF),
            pltpu.VMEM((8, 32, 384), BF),
            pltpu.VMEM((8, 64, 256), BF),
            pltpu.VMEM((8, 48, 256), BF),
            pltpu.SemaphoreType.DMA((4,)),
            pltpu.SemaphoreType.DMA((7,)),
            pltpu.SemaphoreType.DMA((8,)),
            pltpu.SemaphoreType.DMA((8,)),
        ],
        compiler_params=pltpu.CompilerParams(
            collective_id=0, has_side_effects=True, vmem_limit_bytes=32 * 1024 * 1024
        ),
    )(*operands)


def solution(mesh):
    placed = (P("gx", "gy", None), P(), P(), P(), P())
    return jax.shard_map(
        local, mesh=mesh, in_specs=placed, out_specs=P("gx", "gy", None), check_vma=False
    )
```

profile of v0, /device:TPU:1, one launch (start us, length us, event | category | flops | bytes accessed | tf_op | source)
XLA Modules:
  0.0 23.8 jit_solution(434063793987767399)
XLA Ops:
  0.0 23.2 %shard_map.55 = f32[4,4,1024]{2,1,0:T(4,128)S(1)} custom-call(bf16[4,4,1024]{2,1,0:T(4,128)(2,1)} %density.1, bf16[56,64]{1,0:T(8,128)(2,1)} %bitcast.1, bf16[7,7,7,56,56]{4,3,2,1,0:T(8,128)(2,1)} %m2l.1, bf16[3,3,3,64,64]{4,3,2,1,0:T(8,128)(2,1)} %near.1, bf16[56,64]{1,0:T(8,128)(2,1)} %l2p.1), custom_call_target="tpu_custom_call" | custom-call | tf_op jit(solution)/shard_map/pallas_call | solution.py:264
  23.2 0.6 %copy.7 = f32[4,4,1024]{2,1,0:T(4,128)} copy(f32[4,4,1024]{2,1,0:T(4,128)S(1)} %shard_map.55) | data formatting | bytes 131072
where the time goes:
time: 24 us; the launch traced here: 23.8 us
  Pallas kernels  23.2 us (97%)
  local copies, waits for them, and re-layouts  0.63 us (3%)
    pallas_call x1, Pallas kernels, local(): pl.pallas_call(kernel, out_shape=jax.ShapeDtypeStruct(density.shape, F32)...  23.2 us
    unnamed x1, local copies, waits for them, and re-layouts  0.63 us

commit v1 on v0

v1 whole, which is shorter than its diff:
```python
import jax
import jax.numpy as jnp
from jax import lax
from jax.experimental import pallas as pl
from jax.experimental.pallas import tpu as pltpu
from jax.sharding import PartitionSpec as P

BF = jnp.bfloat16
F32 = jnp.float32
MESH = pl.DeviceIdType.MESH
HALO = 2
SIDES = [(dx, dy) for dx in (-1, 0, 1) for dy in (-1, 0, 1) if (dx, dy) != (0, 0)]
SOURCE = {-1: slice(2, 4), 0: slice(2, 6), 1: slice(4, 6)}
TARGET = {-1: slice(6, 8), 0: slice(2, 6), 1: slice(0, 2)}


def near_offset(ox, oy):
    return 2 <= ox <= 4 and 2 <= oy <= 4


def far_tiles():
    classes = {}
    for ox in range(7):
        pars = tuple(p for p in (0, 1) if 0 <= ox - 1 + p <= 5)
        for oy in range(7):
            if oy in (0, 6):
                ys = (1, 3) if oy == 0 else (0, 2)
            else:
                ys = (0, 1, 2, 3)
            for c in (0, 2) if near_offset(ox, oy) else (0, 1, 2):
                classes.setdefault((pars, ys), []).append((ox, oy, c))
    tiles = []
    for (pars, ys), chunks in classes.items():
        for i in range(0, len(chunks), 2):
            tiles.append((pars, ys, chunks[i : i + 2]))
    return tiles


def widen(block):
    rows, lanes = block.shape
    block = jnp.concatenate([block, jnp.zeros((rows, 128 - lanes), BF)], axis=1)
    if rows < 64:
        block = jnp.concatenate([block, jnp.zeros((64 - rows, 128), BF)], axis=0)
    return block


def kernel(
    density, p2m_t, m2l, near, l2p, out,
    raw, cells, table, near_raw, p2m_raw, l2p_raw, wide, near_wide, far_rows, near_rows,
    in_sems, table_sems, send_sems, recv_sems,
):
    gx, gy = lax.axis_index("gx"), lax.axis_index("gy")
    nx, ny = lax.axis_size("gx"), lax.axis_size("gy")

    def present(dx, dy):
        ok = None
        for d, g, n in ((dx, gx, nx), (dy, gy, ny)):
            if d:
                test = (g + d >= 0) & (g + d < n)
                ok = test if ok is None else ok & test
        return ok

    copies_in = [
        pltpu.make_async_copy(density, raw, in_sems.at[0]),
        pltpu.make_async_copy(near, near_raw, in_sems.at[1]),
        pltpu.make_async_copy(p2m_t, p2m_raw, in_sems.at[2]),
        pltpu.make_async_copy(l2p, l2p_raw, in_sems.at[3]),
    ]
    copies_in[0].start()
    barrier = pltpu.get_barrier_semaphore()
    count = jnp.int32(0)
    for dx, dy in SIDES:
        ok = present(dx, dy)
        count = count + ok.astype(jnp.int32)

        @pl.when(ok)
        def _():
            pl.semaphore_signal(
                barrier, inc=1, device_id=(gx + dx, gy + dy), device_id_type=MESH
            )
    for c in copies_in[1:]:
        c.start()
    table_copies = [
        pltpu.make_async_copy(m2l.at[i], table.at[i], table_sems.at[i]) for i in range(7)
    ]
    for c in table_copies:
        c.start()

    for dx, dy in SIDES:
        @pl.when(jnp.logical_not(present(dx, dy)))
        def _():
            ys, xs = TARGET[-dy], TARGET[-dx]
            cells[ys, xs] = jnp.zeros((ys.stop - ys.start, xs.stop - xs.start, 8, 128), BF)

    copies_in[0].wait()
    own = raw[...].astype(F32)
    for y in range(4):
        for x in range(4):
            tile = jnp.concatenate(
                [own[x, y : y + 1, 128 * z : 128 * z + 128] for z in range(8)], axis=0
            )
            cells[HALO + y, HALO + x] = tile.astype(BF)

    pl.semaphore_wait(barrier, count)

    def remote(k):
        dx, dy = SIDES[k]
        return pltpu.make_async_remote_copy(
            src_ref=cells.at[SOURCE[dy], SOURCE[dx]],
            dst_ref=cells.at[TARGET[dy], TARGET[dx]],
            send_sem=send_sems.at[k],
            recv_sem=recv_sems.at[k],
            device_id=(gx + dx, gy + dy),
            device_id_type=MESH,
        )

    for k, (dx, dy) in enumerate(SIDES):
        @pl.when(present(dx, dy))
        def _():
            remote(k).start()

    for c in copies_in[1:]:
        c.wait()
    p2m_block = widen(p2m_raw[...])
    p2m = jnp.concatenate([p2m_block, pltpu.roll(p2m_block, 64, 1)], axis=0)
    l2p_block = jnp.concatenate([widen(l2p_raw[...]), jnp.zeros((64, 128), BF)], axis=0)
    zero_block = jnp.zeros((128, 128), BF)
    l2p_pair = jnp.concatenate(
        [
            jnp.concatenate([l2p_block, zero_block], axis=1),
            jnp.concatenate([zero_block, l2p_block], axis=1),
        ],
        axis=0,
    )

    def widen_near(i, carry):
        for k in range(3):
            near_wide[i, k] = widen(near_raw[i // 3, i % 3, k])
        return carry

    lax.fori_loop(0, 9, widen_near, 0)
    for ox in range(7):
        table_copies[ox].wait()

        def widen_far(oy, carry):
            for k in range(7):
                wide[ox, oy, k] = widen(table[ox, oy, k])
            return carry

        lax.fori_loop(0, 7, widen_far, 0)
        if 2 <= ox <= 4:
            for oy in range(2, 5):
                wide[ox, oy, 2:5] = jnp.zeros((3, 64, 128), BF)

    for k, (dx, dy) in enumerate(SIDES):
        @pl.when(present(-dx, -dy))
        def _():
            remote(k).wait_recv()

    row = lax.broadcasted_iota(jnp.int32, (8, 8, 128), 1)
    half = lax.broadcasted_iota(jnp.int32, (8, 8, 128), 2) < 64

    def below(v):
        return jnp.where(row == 0, 0.0, pltpu.roll(v, 1, 1))

    def above(v):
        return jnp.where(row == 7, 0.0, pltpu.roll(v, 7, 1))

    p2m_pair = jnp.concatenate(
        [
            jnp.concatenate([p2m, zero_block], axis=1),
            jnp.concatenate([zero_block, p2m], axis=1),
        ],
        axis=0,
    )

    def spread(*accs):
        for mxu in range(2):
            pltpu.matmul_push_rhs(p2m_pair, 0, mxu, transpose=True)
        for i in range(4):
            lhs = jnp.concatenate([cells[2 * i + j].reshape(64, 128) for j in range(2)], axis=1)
            pltpu.matmul_acc_lhs(accs[i], lhs, load_staged_rhs=0 if i < 2 else None)
        for i in range(4):
            pair = pltpu.matmul_pop(accs[i])
            for j in range(2):
                y = 2 * i + j
                m = pair[:, 128 * j : 128 * j + 128].reshape(8, 8, 128)
                rows = cells[y].astype(F32)
                for part, v in enumerate((below(m), m, above(m))):
                    for x in range(6):
                        far_rows[y, x, :, 128 * part : 128 * part + 128] = jnp.concatenate(
                            [v[x], v[x + 2]], axis=0
                        ).astype(BF)
                if y in (0, 7):
                    continue
                edge = jnp.where(half, above(rows), below(rows))
                for part, v in enumerate((rows, edge)):
                    for x in range(1, 5):
                        near_rows[y, x - 1, :, 128 * part : 128 * part + 128] = jnp.concatenate(
                            [v[x], v[x + 2]], axis=0
                        ).astype(BF)

    pl.run_scoped(spread, *[pltpu.ACC(i % 2)((64, 256), F32) for i in range(4)])

    def products(*accs):
        acc_far = [accs[0:8], accs[8:16]]
        acc_near = [accs[16:24], accs[24:32]]
        staged = [0, 0]

        def push(rhs, mxu):
            slot = staged[mxu] % 2
            staged[mxu] += 1
            pltpu.matmul_push_rhs(rhs, slot, mxu)
            return slot

        for i in range(9):
            mxu = i % 2
            dx, dy = i // 3, i % 3
            below_w, own_w, above_w = (near_wide[i, k] for k in range(3))
            zero = jnp.zeros((64, 128), BF)
            rhs = jnp.concatenate(
                [
                    jnp.concatenate([own_w, above_w, zero, below_w], axis=0),
                    jnp.concatenate([below_w, own_w, above_w, zero], axis=0),
                ],
                axis=1,
            )
            slot = push(rhs, mxu)
            for y in range(4):
                for par in range(2):
                    pltpu.matmul_acc_lhs(
                        acc_near[mxu][2 * y + par], near_rows[y + dy + 1, dx + par],
                        load_staged_rhs=slot,
                    )
                    slot = None

        def far_rhs(ox, oy, c):
            return jnp.concatenate(
                [
                    wide[ox, oy, 2 * c + 1 : 2 * c + 3].reshape(128, 128),
                    wide[ox, oy, 2 * c : 2 * c + 2].reshape(128, 128),
                ],
                axis=1,
            )

        for i, (pars, ys, chunks) in enumerate(far_tiles()):
            mxu = (i + 1) % 2
            parts = [far_rhs(*chunk) for chunk in chunks]
            if len(parts) == 1:
                parts.append(jnp.zeros((128, 256), BF))
            slot = push(jnp.concatenate(parts, axis=0), mxu)
            for y in ys:
                for par in pars:
                    lhs = [
                        far_rows[y + oy - 1, ox - 1 + par, :, 128 * c : 128 * c + 128]
                        for ox, oy, c in chunks
                    ]
                    if len(lhs) == 1:
                        lhs.append(jnp.zeros((16, 128), BF))
                    pltpu.matmul_acc_lhs(
                        acc_far[mxu][2 * y + par], jnp.concatenate(lhs, axis=1), load_staged_rhs=slot
                    )
                    slot = None

        slot = push(l2p_pair, 0)
        for unit in range(8):
            expansion = pltpu.matmul_pop(acc_far[0][unit]) + pltpu.matmul_pop(acc_far[1][unit])
            pltpu.matmul_acc_lhs(acc_near[0][unit], expansion.astype(BF), load_staged_rhs=slot)
            slot = None
        for y in range(4):
            for par in range(2):
                unit = 2 * y + par
                both = pltpu.matmul_pop(acc_near[0][unit]) + pltpu.matmul_pop(acc_near[1][unit])
                low = lax.broadcasted_iota(jnp.int32, (16, 128), 1) < 64
                value = jnp.where(low, both[:, :128], pltpu.roll(both[:, 128:], 64, 1))
                for i in range(2):
                    for z in range(8):
                        r = 8 * i + z
                        out[2 * i + par, y : y + 1, 128 * z : 128 * z + 128] = value[r : r + 1]
    pl.run_scoped(
        products,
        *[pltpu.ACC(mxu)((16, 256), F32) for _ in range(2) for mxu in range(2) for _ in range(8)],
    )

    for k, (dx, dy) in enumerate(SIDES):
        @pl.when(present(dx, dy))
        def _():
            remote(k).wait_send()


def local(density, p2m_operator, m2l_table, near_table, l2p_operator):
    in_hbm = pl.BlockSpec(memory_space=pltpu.HBM)
    operands = [
        pltpu.with_memory_space_constraint(v, pltpu.HBM)
        for v in (density, p2m_operator.T, m2l_table, near_table, l2p_operator)
    ]
    return pl.pallas_call(
        kernel,
        out_shape=jax.ShapeDtypeStruct(density.shape, F32),
        in_specs=[in_hbm] * 5,
        out_specs=pl.BlockSpec(memory_space=pltpu.VMEM),
        scratch_shapes=[
            pltpu.VMEM((4, 4, 1024), BF),
            pltpu.VMEM((8, 8, 8, 128), BF),
            pltpu.VMEM((7, 7, 7, 56, 56), BF),
            pltpu.VMEM((3, 3, 3, 64, 64), BF),
            pltpu.VMEM((56, 64), BF),
            pltpu.VMEM((56, 64), BF),
            pltpu.VMEM((7, 7, 7, 64, 128), BF),
            pltpu.VMEM((9, 3, 64, 128), BF),
            pltpu.VMEM((8, 6, 16, 384), BF),
            pltpu.VMEM((8, 4, 16, 256), BF),
            pltpu.SemaphoreType.DMA((4,)),
            pltpu.SemaphoreType.DMA((7,)),
            pltpu.SemaphoreType.DMA((8,)),
            pltpu.SemaphoreType.DMA((8,)),
        ],
        compiler_params=pltpu.CompilerParams(
            collective_id=0, has_side_effects=True, vmem_limit_bytes=32 * 1024 * 1024
        ),
    )(*operands)


def solution(mesh):
    placed = (P("gx", "gy", None), P(), P(), P(), P())

    def build(*args):
        with jax.sharding.use_abstract_mesh(mesh.abstract_mesh):
            return jax.shard_map(
                local, mesh=mesh, in_specs=placed, out_specs=P("gx", "gy", None), check_vma=False
            )(*args)

    return build
```

time: 24 us -> 21.2 us (0.88)
  Pallas kernels: 23.2 us -> 20.5 us
    pallas_call x1, Pallas kernels: 23.2 us -> 20.5 us  [local(): pl.pallas_call(kernel, out_shape=jax.ShapeDtypeStruct(density.shape, F32)...]
where the time goes in v1:
time: 21.2 us; the launch traced here: 21.1 us
  Pallas kernels  20.5 us (97%)
  local copies, waits for them, and re-layouts  0.63 us (3%)
    pallas_call x1, Pallas kernels, local(): pl.pallas_call(kernel, out_shape=jax.ShapeDtypeStruct(density.shape, F32)...  20.5 us
    unnamed x1, local copies, waits for them, and re-layouts  0.63 us

profile of v1, /device:TPU:1, one launch (start us, length us, event | category | flops | bytes accessed | tf_op | source)
XLA Modules:
  0.0 21.1 jit_solution(11471834152461768457)
XLA Ops:
  0.0 20.5 %shard_map.55 = f32[4,4,1024]{2,1,0:T(4,128)S(1)} custom-call(bf16[4,4,1024]{2,1,0:T(4,128)(2,1)} %density.1, bf16[56,64]{1,0:T(8,128)(2,1)} %bitcast.1, bf16[7,7,7,56,56]{4,3,2,1,0:T(8,128)(2,1)} %m2l.1, bf16[3,3,3,64,64]{4,3,2,1,0:T(8,128)(2,1)} %near.1, bf16[56,64]{1,0:T(8,128)(2,1)} %l2p.1), custom_call_target="tpu_custom_call" | custom-call | tf_op jit(solution)/shard_map/pallas_call | solution.py:297
  20.5 0.6 %copy.7 = f32[4,4,1024]{2,1,0:T(4,128)} copy(f32[4,4,1024]{2,1,0:T(4,128)S(1)} %shard_map.55) | data formatting | bytes 131072

commit v2 on v0

v2 whole, which is shorter than its diff:
```python
import jax
import jax.numpy as jnp
from jax import lax
from jax.experimental import pallas as pl
from jax.experimental.pallas import tpu as pltpu
from jax.sharding import PartitionSpec as P

BF = jnp.bfloat16
F32 = jnp.float32
MESH = pl.DeviceIdType.MESH
HALO = 2
SIDES = [(dx, dy) for dx in (-1, 0, 1) for dy in (-1, 0, 1) if (dx, dy) != (0, 0)]
SOURCE = {-1: slice(2, 4), 0: slice(2, 6), 1: slice(4, 6)}
TARGET = {-1: slice(6, 8), 0: slice(2, 6), 1: slice(0, 2)}


def near_offset(ox, oy):
    return 2 <= ox <= 4 and 2 <= oy <= 4


def chunks(ox, oy):
    return (0, 2) if near_offset(ox, oy) else (0, 1, 2)


def parities(offset):
    return tuple(p for p in (0, 1) if 0 <= offset - 1 + p <= 5)


def early_columns():
    return {0: ((1, 0),), 1: ((0, 0), (1, 1)), 2: ((0, 1),)}


def late_products():
    classes = {}
    for ox in range(7):
        for oy in range(7):
            units = []
            for t, s in early_columns().get(ox, ()):
                units += [("x", t, p) for p in parities(oy)]
            for t, s in early_columns().get(oy, ()):
                units += [("y", t, p) for p in parities(ox)]
            if units:
                classes.setdefault(tuple(units), []).append((ox, oy))
    return classes


def dot(a, b):
    return jnp.dot(a, b, preferred_element_type=F32)


def widen(block):
    rows, lanes = block.shape
    block = jnp.concatenate([block, jnp.zeros((rows, 128 - lanes), BF)], axis=1)
    if rows < 64:
        block = jnp.concatenate([block, jnp.zeros((64 - rows, 128), BF)], axis=0)
    return block


def swap(block):
    return pltpu.roll(block, 64, 1)


def kernel(
    density, p2m_t, m2l, near, l2p, out,
    raw, cells, table, near_raw, p2m_raw, l2p_raw, weights, near_weights,
    far_rows, near_rows, far_x, far_y, near_x, near_y, total_ref, close_ref,
    in_sems, table_sems, send_sems, recv_sems,
):
    gx, gy = lax.axis_index("gx"), lax.axis_index("gy")
    nx, ny = lax.axis_size("gx"), lax.axis_size("gy")

    def present(dx, dy):
        ok = None
        for d, g, n in ((dx, gx, nx), (dy, gy, ny)):
            if d:
                test = (g + d >= 0) & (g + d < n)
                ok = test if ok is None else ok & test
        return ok

    copies_in = [
        pltpu.make_async_copy(density, raw, in_sems.at[0]),
        pltpu.make_async_copy(near, near_raw, in_sems.at[1]),
        pltpu.make_async_copy(p2m_t, p2m_raw, in_sems.at[2]),
        pltpu.make_async_copy(l2p, l2p_raw, in_sems.at[3]),
    ]
    copies_in[0].start()
    barrier = pltpu.get_barrier_semaphore()
    count = jnp.int32(0)
    for dx, dy in SIDES:
        ok = present(dx, dy)
        count = count + ok.astype(jnp.int32)

        @pl.when(ok)
        def _():
            pl.semaphore_signal(
                barrier, inc=1, device_id=(gx + dx, gy + dy), device_id_type=MESH
            )
    for c in copies_in[1:]:
        c.start()
    table_copies = [
        pltpu.make_async_copy(m2l.at[i], table.at[i], table_sems.at[i]) for i in range(7)
    ]
    for c in table_copies:
        c.start()

    for dx, dy in SIDES:
        @pl.when(jnp.logical_not(present(dx, dy)))
        def _():
            ys, xs = TARGET[-dy], TARGET[-dx]
            cells[ys, xs] = jnp.zeros((ys.stop - ys.start, xs.stop - xs.start, 8, 128), BF)

    copies_in[0].wait()
    own = raw[...].astype(F32)
    for y in range(4):
        for x in range(4):
            tile = jnp.concatenate(
                [own[x, y : y + 1, 128 * z : 128 * z + 128] for z in range(8)], axis=0
            )
            cells[HALO + y, HALO + x] = tile.astype(BF)

    pl.semaphore_wait(barrier, count)

    def remote(k):
        dx, dy = SIDES[k]
        return pltpu.make_async_remote_copy(
            src_ref=cells.at[SOURCE[dy], SOURCE[dx]],
            dst_ref=cells.at[TARGET[dy], TARGET[dx]],
            send_sem=send_sems.at[k],
            recv_sem=recv_sems.at[k],
            device_id=(gx + dx, gy + dy),
            device_id_type=MESH,
        )

    for k, (dx, dy) in enumerate(SIDES):
        @pl.when(present(dx, dy))
        def _():
            remote(k).start()

    def arrive(sides):
        for k, (dx, dy) in enumerate(SIDES):
            if (dx, dy) in sides:
                @pl.when(present(-dx, -dy))
                def _():
                    remote(k).wait_recv()

    for c in copies_in[1:]:
        c.wait()
    p2m_block = widen(p2m_raw[...])
    p2m = jnp.concatenate([p2m_block, swap(p2m_block)], axis=0)
    l2p_block = widen(l2p_raw[...])
    l2p_pair = jnp.concatenate([l2p_block, swap(l2p_block)], axis=0)
    low = lax.broadcasted_iota(jnp.int32, (64, 128), 1) < 64

    def build_near(i, carry):
        a, b, c = (widen(near_raw[i // 3, i % 3, k]) for k in range(3))
        near_weights[i, 0:64] = jnp.where(low, b, swap(a))
        near_weights[i, 64:128] = jnp.where(low, c, swap(b))
        near_weights[i, 128:192] = swap(c)
        near_weights[i, 192:256] = a
        return carry

    lax.fori_loop(0, 9, build_near, 0)

    for ox in range(7):
        table_copies[ox].wait()

        def build(oy, carry):
            blocks = [widen(table[ox, oy, k]) for k in range(7)]
            for k in range(6):
                weights[ox, oy, 64 * k : 64 * k + 64] = jnp.where(
                    low, blocks[k + 1], swap(blocks[k])
                )
            return carry

        lax.fori_loop(0, 7, build, 0)
        if 2 <= ox <= 4:
            def build_close(oy, carry):
                weights[ox, oy, 64:128] = swap(widen(table[ox, oy, 1]))
                weights[ox, oy, 256:320] = widen(table[ox, oy, 5])
                return carry

            lax.fori_loop(2, 5, build_close, 0)

    def far_weights(pairs):
        return jnp.concatenate(
            [
                weights[ox, oy, 128 * c : 128 * c + 128]
                for ox, oy in pairs
                for c in chunks(ox, oy)
            ],
            axis=0,
        )

    def shifted(v):
        row = lax.broadcasted_iota(jnp.int32, v.shape, 1)
        below = jnp.where(row == 0, 0.0, pltpu.roll(v, 1, 1))
        above = jnp.where(row == 7, 0.0, pltpu.roll(v, 7, 1))
        return below, v, above

    def multipoles(columns):
        n = columns.shape[0]
        m = lax.dot_general(
            columns.reshape(8 * n, 128), p2m, (((1,), (1,)), ((), ())),
            preferred_element_type=F32,
        )
        return shifted(m.reshape(n, 8, 128))

    def neighbours(columns):
        below, own_rows, above = shifted(columns.astype(F32))
        half = lax.broadcasted_iota(jnp.int32, own_rows.shape, 2) < 64
        return own_rows, jnp.where(half, above, below)

    def pair(a, b):
        return jnp.concatenate([a, b], axis=0).astype(BF)

    zero_rows = jnp.zeros((8, 128), F32)

    arrive(((-1, 0), (0, -1), (-1, -1)))
    far_rows[0:2] = jnp.zeros((2, 6, 16, 384), BF)
    near_rows[0] = jnp.zeros((4, 16, 256), BF)

    def spread(y, carry):
        columns = cells[y, 2:8]
        for part, v in enumerate(multipoles(columns)):
            ln = slice(128 * part, 128 * part + 128)
            for x in range(6):
                first = v[x - 2] if x >= 2 else zero_rows
                far_rows[y, x, :, ln] = pair(first, v[x])
        for part, v in enumerate(neighbours(columns[0:5])):
            ln = slice(128 * part, 128 * part + 128)
            for x in range(1, 5):
                first = v[x - 2] if x >= 2 else zero_rows
                near_rows[y - 1, x - 1, :, ln] = pair(first, v[x])
        return carry

    lax.fori_loop(2, 8, spread, 0)

    close = jnp.zeros((128, 128), F32)
    for dx in range(3):
        for dy in range(3):
            close += dot(
                near_rows[dy : dy + 4, dx : dx + 2].reshape(128, 256), near_weights[3 * dx + dy]
            )
    close_ref[...] = close

    def place(value, ys, pars):
        i = 0
        for y in ys:
            for par in pars:
                total_ref[y, par] += value[16 * i : 16 * i + 16]
                i += 1

    total_ref[...] = jnp.zeros_like(total_ref)
    for pars in ((0, 1), (1,), (0,)):
        for ys, oys in (((0, 1, 2, 3), range(1, 6)), ((1, 3), (0,)), ((0, 2), (6,))):
            acc = jnp.zeros((16 * len(ys) * len(pars), 128), F32)
            for ox in range(7):
                if parities(ox) != pars:
                    continue
                x0 = ox - 1 + pars[0]
                for oy in oys:
                    lhs = jnp.concatenate(
                        [
                            jnp.concatenate(
                                [
                                    far_rows[y + oy - 1, x0 : x0 + len(pars), :, 128 * c : 128 * c + 128]
                                    for y in ys
                                ],
                                axis=0,
                            ).reshape(16 * len(ys) * len(pars), 128)
                            for c in chunks(ox, oy)
                        ],
                        axis=1,
                    )
                    acc += dot(lhs, far_weights([(ox, oy)]))
            place(acc, ys, pars)

    arrive(((1, 0), (0, 1), (1, 1), (1, -1), (-1, 1)))
    columns = cells[:, 0:2].reshape(16, 8, 128)
    for part, v in enumerate(multipoles(columns)):
        ln = slice(128 * part, 128 * part + 128)
        for x in range(2):
            for y in range(6):
                far_x[x, y, :, ln] = pair(v[2 * y + x], v[2 * y + 4 + x])
    for part, v in enumerate(neighbours(cells[1:7, 1])):
        ln = slice(128 * part, 128 * part + 128)
        for y in range(4):
            near_x[y, :, ln] = pair(v[y], v[y + 2])
    columns = cells[0:2, 2:8].reshape(12, 8, 128)
    for part, v in enumerate(multipoles(columns)):
        ln = slice(128 * part, 128 * part + 128)
        for y in range(2):
            for x in range(6):
                first = v[6 * y + x - 2] if x >= 2 else zero_rows
                far_y[y, x, :, ln] = pair(first, v[6 * y + x])
    for part, v in enumerate(neighbours(cells[1, 2:7])):
        ln = slice(128 * part, 128 * part + 128)
        for x in range(1, 5):
            first = v[x - 2] if x >= 2 else zero_rows
            near_y[x - 1, :, ln] = pair(first, v[x])

    near_late = {}
    for axis, ref, places in (("x", near_x, (0, 1, 2)), ("y", near_y, (0, 3, 6))):
        lhs = jnp.concatenate([ref[d : d + 2].reshape(32, 256) for d in range(3)], axis=1)
        rhs = jnp.concatenate([near_weights[i] for i in places], axis=0)
        near_late[axis] = dot(lhs, rhs)

    late = {}
    for units, pairs in late_products().items():
        columns = []
        for ox, oy in pairs:
            for c in chunks(ox, oy):
                ln = slice(128 * c, 128 * c + 128)
                rows = []
                for axis, t, p in units:
                    if axis == "x":
                        rows.append(far_x[t + ox - 1, oy - 1 + p, :, ln])
                    else:
                        rows.append(far_y[t + oy - 1, ox - 1 + p, :, ln])
                columns.append(jnp.concatenate(rows, axis=0))
        value = dot(jnp.concatenate(columns, axis=1), far_weights(pairs))
        for i, unit in enumerate(units):
            part = value[16 * i : 16 * i + 16]
            late[unit] = late[unit] + part if unit in late else part

    def eight(value, i):
        return value[8 * i : 8 * i + 8]

    expansion = []
    for y in range(4):
        for x in range(4):
            value = eight(total_ref[y, x % 2], x // 2)
            if x < 2:
                value = value + eight(late["x", x, y % 2], y // 2)
            if y < 2:
                value = value + eight(late["y", y, x % 2], x // 2)
            expansion.append(value)
    distant = dot(jnp.concatenate(expansion, axis=0).astype(BF), l2p_pair)
    for y in range(4):
        for x in range(4):
            value = eight(distant, 4 * y + x) + eight(close_ref[...], 4 * y + 2 * (x % 2) + x // 2)
            if x == 0:
                value = value + eight(near_late["x"], 2 * (y % 2) + y // 2)
            if y == 0:
                value = value + eight(near_late["y"], 2 * (x % 2) + x // 2)
            for z in range(8):
                out[x, y : y + 1, 128 * z : 128 * z + 128] = value[z : z + 1]

    for k, (dx, dy) in enumerate(SIDES):
        @pl.when(present(dx, dy))
        def _():
            remote(k).wait_send()


def local(density, p2m_operator, m2l_table, near_table, l2p_operator):
    in_hbm = pl.BlockSpec(memory_space=pltpu.HBM)
    operands = [
        pltpu.with_memory_space_constraint(v, pltpu.HBM)
        for v in (density, p2m_operator.T, m2l_table, near_table, l2p_operator)
    ]
    return pl.pallas_call(
        kernel,
        out_shape=jax.ShapeDtypeStruct(density.shape, F32),
        in_specs=[in_hbm] * 5,
        out_specs=pl.BlockSpec(memory_space=pltpu.VMEM),
        scratch_shapes=[
            pltpu.VMEM((4, 4, 1024), BF),
            pltpu.VMEM((8, 8, 8, 128), BF),
            pltpu.VMEM((7, 7, 7, 56, 56), BF),
            pltpu.VMEM((3, 3, 3, 64, 64), BF),
            pltpu.VMEM((56, 64), BF),
            pltpu.VMEM((56, 64), BF),
            pltpu.VMEM((7, 7, 384, 128), BF),
            pltpu.VMEM((9, 256, 128), BF),
            pltpu.VMEM((8, 6, 16, 384), BF),
            pltpu.VMEM((7, 4, 16, 256), BF),
            pltpu.VMEM((2, 6, 16, 384), BF),
            pltpu.VMEM((2, 6, 16, 384), BF),
            pltpu.VMEM((4, 16, 256), BF),
            pltpu.VMEM((4, 16, 256), BF),
            pltpu.VMEM((4, 2, 16, 128), F32),
            pltpu.VMEM((128, 128), F32),
            pltpu.SemaphoreType.DMA((4,)),
            pltpu.SemaphoreType.DMA((7,)),
            pltpu.SemaphoreType.DMA((8,)),
            pltpu.SemaphoreType.DMA((8,)),
        ],
        compiler_params=pltpu.CompilerParams(
            collective_id=0, has_side_effects=True, vmem_limit_bytes=32 * 1024 * 1024
        ),
    )(*operands)


def solution(mesh):
    placed = (P("gx", "gy", None), P(), P(), P(), P())
    return jax.shard_map(
        local, mesh=mesh, in_specs=placed, out_specs=P("gx", "gy", None), check_vma=False
    )
```

time: 24 us -> 25.3 us (1.054)
  Pallas kernels: 23.2 us -> 24.5 us
    pallas_call x1, Pallas kernels: 23.2 us -> 24.5 us  [local(): pl.pallas_call(kernel, out_shape=jax.ShapeDtypeStruct(density.shape, F32)...]
where the time goes in v2:
time: 25.3 us; the launch traced here: 25.1 us
  Pallas kernels  24.5 us (97%)
  local copies, waits for them, and re-layouts  0.63 us (2%)
    pallas_call x1, Pallas kernels, local(): pl.pallas_call(kernel, out_shape=jax.ShapeDtypeStruct(density.shape, F32)...  24.5 us
    unnamed x1, local copies, waits for them, and re-layouts  0.63 us

profile of v2, /device:TPU:1, one launch (start us, length us, event | category | flops | bytes accessed | tf_op | source)
XLA Modules:
  0.0 25.1 jit_solution(10450260958219299363)
XLA Ops:
  0.0 24.5 %shard_map.55 = f32[4,4,1024]{2,1,0:T(4,128)S(1)} custom-call(bf16[4,4,1024]{2,1,0:T(4,128)(2,1)} %density.1, bf16[56,64]{1,0:T(8,128)(2,1)} %bitcast.1, bf16[7,7,7,56,56]{4,3,2,1,0:T(8,128)(2,1)} %m2l.1, bf16[3,3,3,64,64]{4,3,2,1,0:T(8,128)(2,1)} %near.1, bf16[56,64]{1,0:T(8,128)(2,1)} %l2p.1), custom_call_target="tpu_custom_call" | custom-call | tf_op jit(solution)/shard_map/pallas_call | solution.py:361
  24.5 0.6 %copy.7 = f32[4,4,1024]{2,1,0:T(4,128)} copy(f32[4,4,1024]{2,1,0:T(4,128)S(1)} %shard_map.55) | data formatting | bytes 131072

commit v3 on v2

--- a/solution.py
+++ b/solution.py
@@ -9,7 +9,8 @@
 F32 = jnp.float32
 MESH = pl.DeviceIdType.MESH
 HALO = 2
-SIDES = [(dx, dy) for dx in (-1, 0, 1) for dy in (-1, 0, 1) if (dx, dy) != (0, 0)]
+SIDES = [(1, 0), (0, 1), (1, 1), (1, -1), (-1, 1), (-1, 0), (0, -1), (-1, -1)]
+LOWER = [(-1, 0), (0, -1), (-1, -1)]
 SOURCE = {-1: slice(2, 4), 0: slice(2, 6), 1: slice(4, 6)}
 TARGET = {-1: slice(6, 8), 0: slice(2, 6), 1: slice(0, 2)}
 
@@ -64,7 +65,7 @@
     density, p2m_t, m2l, near, l2p, out,
     raw, cells, table, near_raw, p2m_raw, l2p_raw, weights, near_weights,
     far_rows, near_rows, far_x, far_y, near_x, near_y, total_ref, close_ref,
-    in_sems, table_sems, send_sems, recv_sems,
+    in_sems, table_sems, send_sems, recv_sems, ready,
 ):
     gx, gy = lax.axis_index("gx"), lax.axis_index("gy")
     nx, ny = lax.axis_size("gx"), lax.axis_size("gy")
@@ -85,12 +86,18 @@
     ]
     copies_in[0].start()
     barrier = pltpu.get_barrier_semaphore()
+
+    def leads(dx, dy):
+        return (gx + dx == 0) & (gy + dy == 0)
+
+    def beside(dx, dy):
+        return present(dx, dy) & jnp.logical_not(leads(dx, dy))
+
     count = jnp.int32(0)
     for dx, dy in SIDES:
-        ok = present(dx, dy)
-        count = count + ok.astype(jnp.int32)
-
-        @pl.when(ok)
+        count = count + beside(dx, dy).astype(jnp.int32)
+
+        @pl.when(present(dx, dy) & jnp.logical_not(leads(0, 0)))
         def _():
             pl.semaphore_signal(
                 barrier, inc=1, device_id=(gx + dx, gy + dy), device_id_type=MESH
@@ -119,6 +126,12 @@
             cells[HALO + y, HALO + x] = tile.astype(BF)
 
     pl.semaphore_wait(barrier, count)
+    for dx, dy in LOWER:
+        @pl.when(leads(0, 0) & present(-dx, -dy))
+        def _():
+            pl.semaphore_signal(
+                ready, inc=1, device_id=(gx - dx, gy - dy), device_id_type=MESH
+            )
 
     def remote(k):
         dx, dy = SIDES[k]
@@ -132,7 +145,7 @@
         )
 
     for k, (dx, dy) in enumerate(SIDES):
-        @pl.when(present(dx, dy))
+        @pl.when(beside(dx, dy))
         def _():
             remote(k).start()
 
@@ -215,7 +228,7 @@
 
     zero_rows = jnp.zeros((8, 128), F32)
 
-    arrive(((-1, 0), (0, -1), (-1, -1)))
+    arrive(LOWER)
     far_rows[0:2] = jnp.zeros((2, 6, 16, 384), BF)
     near_rows[0] = jnp.zeros((4, 16, 256), BF)
 
@@ -275,7 +288,13 @@
                     acc += dot(lhs, far_weights([(ox, oy)]))
             place(acc, ys, pars)
 
-    arrive(((1, 0), (0, 1), (1, 1), (1, -1), (-1, 1)))
+    for k, (dx, dy) in enumerate(SIDES):
+        if (dx, dy) in LOWER:
+            @pl.when(leads(dx, dy))
+            def _():
+                pl.semaphore_wait(ready, 1)
+                remote(k).start()
+    arrive(tuple(side for side in SIDES if side not in LOWER))
     columns = cells[:, 0:2].reshape(16, 8, 128)
     for part, v in enumerate(multipoles(columns)):
         ln = slice(128 * part, 128 * part + 128)
@@ -384,6 +403,7 @@
             pltpu.SemaphoreType.DMA((7,)),
             pltpu.SemaphoreType.DMA((8,)),
             pltpu.SemaphoreType.DMA((8,)),
+            pltpu.SemaphoreType.REGULAR,
         ],
         compiler_params=pltpu.CompilerParams(
             collective_id=0, has_side_effects=True, vmem_limit_bytes=32 * 1024 * 1024

time: 25.3 us -> 18.7 us (0.74)
  the two profiles are of different devices: /device:TPU:1 before, /device:TPU:9 now
where the time goes in v3:
time: 18.7 us; the launch traced here: 18.5 us
  Pallas kernels  17.9 us (96%)
  local copies, waits for them, and re-layouts  0.63 us (3%)
    pallas_call x1, Pallas kernels, local(): pl.pallas_call(kernel, out_shape=jax.ShapeDtypeStruct(density.shape, F32)...  17.9 us
    unnamed x1, local copies, waits for them, and re-layouts  0.63 us

profile of v3, /device:TPU:9, one launch (start us, length us, event | category | flops | bytes accessed | tf_op | source)
XLA Modules:
  0.0 18.5 jit_solution(2469216810686312167)
XLA Ops:
  0.0 17.9 %shard_map.55 = f32[4,4,1024]{2,1,0:T(4,128)S(1)} custom-call(bf16[4,4,1024]{2,1,0:T(4,128)(2,1)} %density.1, bf16[56,64]{1,0:T(8,128)(2,1)} %bitcast.1, bf16[7,7,7,56,56]{4,3,2,1,0:T(8,128)(2,1)} %m2l.1, bf16[3,3,3,64,64]{4,3,2,1,0:T(8,128)(2,1)} %near.1, bf16[56,64]{1,0:T(8,128)(2,1)} %l2p.1), custom_call_target="tpu_custom_call" | custom-call | tf_op jit(solution)/shard_map/pallas_call | solution.py:380
  17.9 0.6 %copy.7 = f32[4,4,1024]{2,1,0:T(4,128)} copy(f32[4,4,1024]{2,1,0:T(4,128)S(1)} %shard_map.55) | data formatting | bytes 131072

commit v4 on v3

--- a/solution.py
+++ b/solution.py
@@ -172,7 +172,7 @@
         near_weights[i, 192:256] = a
         return carry
 
-    lax.fori_loop(0, 9, build_near, 0)
+    lax.fori_loop(0, 9, build_near, 0, unroll=9)
 
     for ox in range(7):
         table_copies[ox].wait()
@@ -185,14 +185,14 @@
                 )
             return carry
 
-        lax.fori_loop(0, 7, build, 0)
+        lax.fori_loop(0, 7, build, 0, unroll=7)
         if 2 <= ox <= 4:
             def build_close(oy, carry):
                 weights[ox, oy, 64:128] = swap(widen(table[ox, oy, 1]))
                 weights[ox, oy, 256:320] = widen(table[ox, oy, 5])
                 return carry
 
-            lax.fori_loop(2, 5, build_close, 0)
+            lax.fori_loop(2, 5, build_close, 0, unroll=3)
 
     def far_weights(pairs):
         return jnp.concatenate(
@@ -246,7 +246,7 @@
                 near_rows[y - 1, x - 1, :, ln] = pair(first, v[x])
         return carry
 
-    lax.fori_loop(2, 8, spread, 0)
+    lax.fori_loop(2, 8, spread, 0, unroll=6)
 
     close = jnp.zeros((128, 128), F32)
     for dx in range(3):

time: 18.7 us -> 18.7 us (level)
  no operation moved by 1% of the time
where the time goes in v4:
time: 18.7 us; the launch traced here: 18.5 us
  Pallas kernels  17.9 us (96%)
  local copies, waits for them, and re-layouts  0.63 us (3%)
    pallas_call x1, Pallas kernels, local(): pl.pallas_call(kernel, out_shape=jax.ShapeDtypeStruct(density.shape, F32)...  17.9 us
    unnamed x1, local copies, waits for them, and re-layouts  0.63 us

profile of v4, /device:TPU:9, one launch (start us, length us, event | category | flops | bytes accessed | tf_op | source)
XLA Modules:
  0.0 18.5 jit_solution(11286595336166193448)
XLA Ops:
  0.0 17.9 %shard_map.55 = f32[4,4,1024]{2,1,0:T(4,128)S(1)} custom-call(bf16[4,4,1024]{2,1,0:T(4,128)(2,1)} %density.1, bf16[56,64]{1,0:T(8,128)(2,1)} %bitcast.1, bf16[7,7,7,56,56]{4,3,2,1,0:T(8,128)(2,1)} %m2l.1, bf16[3,3,3,64,64]{4,3,2,1,0:T(8,128)(2,1)} %near.1, bf16[56,64]{1,0:T(8,128)(2,1)} %l2p.1), custom_call_target="tpu_custom_call" | custom-call | tf_op jit(solution)/shard_map/pallas_call | solution.py:380
  17.9 0.6 %copy.7 = f32[4,4,1024]{2,1,0:T(4,128)} copy(f32[4,4,1024]{2,1,0:T(4,128)S(1)} %shard_map.55) | data formatting | bytes 131072

commit v5 on v4

--- a/solution.py
+++ b/solution.py
@@ -31,17 +31,16 @@
     return {0: ((1, 0),), 1: ((0, 0), (1, 1)), 2: ((0, 1),)}
 
 
-def late_products():
+def late_products(axis):
     classes = {}
     for ox in range(7):
         for oy in range(7):
-            units = []
-            for t, s in early_columns().get(ox, ()):
-                units += [("x", t, p) for p in parities(oy)]
-            for t, s in early_columns().get(oy, ()):
-                units += [("y", t, p) for p in parities(ox)]
+            along, across = (ox, oy) if axis == "x" else (oy, ox)
+            units = tuple(
+                (t, s - t, p) for t, s in early_columns().get(along, ()) for p in parities(across)
+            )
             if units:
-                classes.setdefault(tuple(units), []).append((ox, oy))
+                classes.setdefault(units, []).append((ox, oy))
     return classes
 
 
@@ -65,6 +64,7 @@
     density, p2m_t, m2l, near, l2p, out,
     raw, cells, table, near_raw, p2m_raw, l2p_raw, weights, near_weights,
     far_rows, near_rows, far_x, far_y, near_x, near_y, total_ref, close_ref,
+    far_late_x, far_late_y, near_late_x, near_late_y,
     in_sems, table_sems, send_sems, recv_sems, ready,
 ):
     gx, gy = lax.axis_index("gx"), lax.axis_index("gy")
@@ -294,53 +294,74 @@
             def _():
                 pl.semaphore_wait(ready, 1)
                 remote(k).start()
-    arrive(tuple(side for side in SIDES if side not in LOWER))
-    columns = cells[:, 0:2].reshape(16, 8, 128)
-    for part, v in enumerate(multipoles(columns)):
-        ln = slice(128 * part, 128 * part + 128)
-        for x in range(2):
-            for y in range(6):
-                far_x[x, y, :, ln] = pair(v[2 * y + x], v[2 * y + 4 + x])
-    for part, v in enumerate(neighbours(cells[1:7, 1])):
-        ln = slice(128 * part, 128 * part + 128)
-        for y in range(4):
-            near_x[y, :, ln] = pair(v[y], v[y + 2])
-    columns = cells[0:2, 2:8].reshape(12, 8, 128)
-    for part, v in enumerate(multipoles(columns)):
-        ln = slice(128 * part, 128 * part + 128)
-        for y in range(2):
-            for x in range(6):
-                first = v[6 * y + x - 2] if x >= 2 else zero_rows
-                far_y[y, x, :, ln] = pair(first, v[6 * y + x])
-    for part, v in enumerate(neighbours(cells[1, 2:7])):
-        ln = slice(128 * part, 128 * part + 128)
-        for x in range(1, 5):
-            first = v[x - 2] if x >= 2 else zero_rows
-            near_y[x - 1, :, ln] = pair(first, v[x])
-
-    near_late = {}
-    for axis, ref, places in (("x", near_x, (0, 1, 2)), ("y", near_y, (0, 3, 6))):
-        lhs = jnp.concatenate([ref[d : d + 2].reshape(32, 256) for d in range(3)], axis=1)
+
+    def late(axis, far_ref, near_ref, far_late, near_late):
+        places = (0, 1, 2) if axis == "x" else (0, 3, 6)
+        lhs = jnp.concatenate([near_ref[d : d + 2].reshape(32, 256) for d in range(3)], axis=1)
         rhs = jnp.concatenate([near_weights[i] for i in places], axis=0)
-        near_late[axis] = dot(lhs, rhs)
-
-    late = {}
-    for units, pairs in late_products().items():
-        columns = []
-        for ox, oy in pairs:
-            for c in chunks(ox, oy):
-                ln = slice(128 * c, 128 * c + 128)
-                rows = []
-                for axis, t, p in units:
-                    if axis == "x":
-                        rows.append(far_x[t + ox - 1, oy - 1 + p, :, ln])
-                    else:
-                        rows.append(far_y[t + oy - 1, ox - 1 + p, :, ln])
-                columns.append(jnp.concatenate(rows, axis=0))
-        value = dot(jnp.concatenate(columns, axis=1), far_weights(pairs))
-        for i, unit in enumerate(units):
-            part = value[16 * i : 16 * i + 16]
-            late[unit] = late[unit] + part if unit in late else part
+        near_late[...] = dot(lhs, rhs)
+        sums = {}
+        for units, pairs in late_products(axis).items():
+            columns = []
+            for ox, oy in pairs:
+                across = oy if axis == "x" else ox
+                for c in chunks(ox, oy):
+                    ln = slice(128 * c, 128 * c + 128)
+                    columns.append(
+                        jnp.concatenate(
+                            [far_ref[t + d, across - 1 + p, :, ln] for t, d, p in units], axis=0
+                        )
+                    )
+            value = dot(jnp.concatenate(columns, axis=1), far_weights(pairs))
+            for i, (t, _, p) in enumerate(units):
+                part = value[16 * i : 16 * i + 16]
+                sums[t, p] = sums[t, p] + part if (t, p) in sums else part
+        for t, p in sums:
+            far_late[t, p] = sums[t, p]
+
+    arrive([side for side in SIDES if side in ((0, 1), (-1, 1))])
+
+    @pl.when(gy == 0)
+    def _():
+        far_late_y[...] = jnp.zeros_like(far_late_y)
+        near_late_y[...] = jnp.zeros_like(near_late_y)
+
+    @pl.when(gy > 0)
+    def _():
+        columns = cells[0:2, 2:8].reshape(12, 8, 128)
+        for part, v in enumerate(multipoles(columns)):
+            ln = slice(128 * part, 128 * part + 128)
+            for y in range(2):
+                for x in range(6):
+                    first = v[6 * y + x - 2] if x >= 2 else zero_rows
+                    far_y[y, x, :, ln] = pair(first, v[6 * y + x])
+        for part, v in enumerate(neighbours(cells[1, 2:7])):
+            ln = slice(128 * part, 128 * part + 128)
+            for x in range(1, 5):
+                first = v[x - 2] if x >= 2 else zero_rows
+                near_y[x - 1, :, ln] = pair(first, v[x])
+        late("y", far_y, near_y, far_late_y, near_late_y)
+
+    arrive([side for side in SIDES if side in ((1, 0), (1, 1), (1, -1))])
+
+    @pl.when(gx == 0)
+    def _():
+        far_late_x[...] = jnp.zeros_like(far_late_x)
+        near_late_x[...] = jnp.zeros_like(near_late_x)
+
+    @pl.when(gx > 0)
+    def _():
+        columns = cells[:, 0:2].reshape(16, 8, 128)
+        for part, v in enumerate(multipoles(columns)):
+            ln = slice(128 * part, 128 * part + 128)
+            for x in range(2):
+                for y in range(6):
+                    far_x[x, y, :, ln] = pair(v[2 * y + x], v[2 * y + 4 + x])
+        for part, v in enumerate(neighbours(cells[1:7, 1])):
+            ln = slice(128 * part, 128 * part + 128)
+            for y in range(4):
+                near_x[y, :, ln] = pair(v[y], v[y + 2])
+        late("x", far_x, near_x, far_late_x, near_late_x)
 
     def eight(value, i):
         return value[8 * i : 8 * i + 8]
@@ -350,18 +371,18 @@
         for x in range(4):
             value = eight(total_ref[y, x % 2], x // 2)
             if x < 2:
-                value = value + eight(late["x", x, y % 2], y // 2)
+                value = value + far_late_x[x, y % 2, 8 * (y // 2) : 8 * (y // 2) + 8]
             if y < 2:
-                value = value + eight(late["y", y, x % 2], x // 2)
+                value = value + far_late_y[y, x % 2, 8 * (x // 2) : 8 * (x // 2) + 8]
             expansion.append(value)
     distant = dot(jnp.concatenate(expansion, axis=0).astype(BF), l2p_pair)
     for y in range(4):
         for x in range(4):
             value = eight(distant, 4 * y + x) + eight(close_ref[...], 4 * y + 2 * (x % 2) + x // 2)
             if x == 0:
-                value = value + eight(near_late["x"], 2 * (y % 2) + y // 2)
+                value = value + eight(near_late_x[...], 2 * (y % 2) + y // 2)
             if y == 0:
-                value = value + eight(near_late["y"], 2 * (x % 2) + x // 2)
+                value = value + eight(near_late_y[...], 2 * (x % 2) + x // 2)
             for z in range(8):
                 out[x, y : y + 1, 128 * z : 128 * z + 128] = value[z : z + 1]
 
@@ -399,6 +420,10 @@
             pltpu.VMEM((4, 16, 256), BF),
             pltpu.VMEM((4, 2, 16, 128), F32),
             pltpu.VMEM((128, 128), F32),
+            pltpu.VMEM((2, 2, 16, 128), F32),
+            pltpu.VMEM((2, 2, 16, 128), F32),
+            pltpu.VMEM((32, 128), F32),
+            pltpu.VMEM((32, 128), F32),
             pltpu.SemaphoreType.DMA((4,)),
             pltpu.SemaphoreType.DMA((7,)),
             pltpu.SemaphoreType.DMA((8,)),

time: 18.7 us -> 18.4 us (0.984)
  Pallas kernels: 17.9 us -> 17.7 us
    pallas_call x1, Pallas kernels: 17.9 us -> 17.7 us  [local(): pl.pallas_call(kernel, out_shape=jax.ShapeDtypeStruct(density.shape, F32)...]
where the time goes in v5:
time: 18.4 us; the launch traced here: 18.3 us
  Pallas kernels  17.7 us (96%)
  local copies, waits for them, and re-layouts  0.63 us (3%)
    pallas_call x1, Pallas kernels, local(): pl.pallas_call(kernel, out_shape=jax.ShapeDtypeStruct(density.shape, F32)...  17.7 us
    unnamed x1, local copies, waits for them, and re-layouts  0.63 us

profile of v5, /device:TPU:9, one launch (start us, length us, event | category | flops | bytes accessed | tf_op | source)
XLA Modules:
  0.0 18.3 jit_solution(1165665571444545465)
XLA Ops:
  0.0 17.7 %shard_map.55 = f32[4,4,1024]{2,1,0:T(4,128)S(1)} custom-call(bf16[4,4,1024]{2,1,0:T(4,128)(2,1)} %density.1, bf16[56,64]{1,0:T(8,128)(2,1)} %bitcast.1, bf16[7,7,7,56,56]{4,3,2,1,0:T(8,128)(2,1)} %m2l.1, bf16[3,3,3,64,64]{4,3,2,1,0:T(8,128)(2,1)} %near.1, bf16[56,64]{1,0:T(8,128)(2,1)} %l2p.1), custom_call_target="tpu_custom_call" | custom-call | tf_op jit(solution)/shard_map/pallas_call | solution.py:401
  17.7 0.6 %copy.7 = f32[4,4,1024]{2,1,0:T(4,128)} copy(f32[4,4,1024]{2,1,0:T(4,128)S(1)} %shard_map.55) | data formatting | bytes 131072

commit v6 on v5

--- a/solution.py
+++ b/solution.py
@@ -9,9 +9,10 @@
 F32 = jnp.float32
 MESH = pl.DeviceIdType.MESH
 HALO = 2
-SIDES = [(1, 0), (0, 1), (1, 1), (1, -1), (-1, 1), (-1, 0), (0, -1), (-1, -1)]
+SIDES = [(1, 1), (0, 1), (1, 0), (1, -1), (-1, 1), (-1, 0), (0, -1), (-1, -1)]
 LOWER = [(-1, 0), (0, -1), (-1, -1)]
 SOURCE = {-1: slice(2, 4), 0: slice(2, 6), 1: slice(4, 6)}
+RAW = {0: slice(0, 4), 1: slice(2, 4)}
 TARGET = {-1: slice(6, 8), 0: slice(2, 6), 1: slice(0, 2)}
 
 
@@ -64,9 +65,10 @@
     density, p2m_t, m2l, near, l2p, out,
     raw, cells, table, near_raw, p2m_raw, l2p_raw, weights, near_weights,
     far_rows, near_rows, far_x, far_y, near_x, near_y, total_ref, close_ref,
-    far_late_x, far_late_y, near_late_x, near_late_y,
+    far_late_x, far_late_y, near_late_x, near_late_y, raw_corner, raw_y, raw_x,
     in_sems, table_sems, send_sems, recv_sems, ready,
 ):
+    raw_in = [raw_corner, raw_y, raw_x]
     gx, gy = lax.axis_index("gx"), lax.axis_index("gy")
     nx, ny = lax.axis_size("gx"), lax.axis_size("gy")
 
@@ -102,37 +104,6 @@
             pl.semaphore_signal(
                 barrier, inc=1, device_id=(gx + dx, gy + dy), device_id_type=MESH
             )
-    for c in copies_in[1:]:
-        c.start()
-    table_copies = [
-        pltpu.make_async_copy(m2l.at[i], table.at[i], table_sems.at[i]) for i in range(7)
-    ]
-    for c in table_copies:
-        c.start()
-
-    for dx, dy in SIDES:
-        @pl.when(jnp.logical_not(present(dx, dy)))
-        def _():
-            ys, xs = TARGET[-dy], TARGET[-dx]
-            cells[ys, xs] = jnp.zeros((ys.stop - ys.start, xs.stop - xs.start, 8, 128), BF)
-
-    copies_in[0].wait()
-    own = raw[...].astype(F32)
-    for y in range(4):
-        for x in range(4):
-            tile = jnp.concatenate(
-                [own[x, y : y + 1, 128 * z : 128 * z + 128] for z in range(8)], axis=0
-            )
-            cells[HALO + y, HALO + x] = tile.astype(BF)
-
-    pl.semaphore_wait(barrier, count)
-    for dx, dy in LOWER:
-        @pl.when(leads(0, 0) & present(-dx, -dy))
-        def _():
-            pl.semaphore_signal(
-                ready, inc=1, device_id=(gx - dx, gy - dy), device_id_type=MESH
-            )
-
     def remote(k):
         dx, dy = SIDES[k]
         return pltpu.make_async_remote_copy(
@@ -144,17 +115,81 @@
             device_id_type=MESH,
         )
 
+    def straight(k):
+        dx, dy = SIDES[k]
+        xs, ys = RAW[dx], RAW[dy]
+        return pltpu.make_async_remote_copy(
+            src_ref=density.at[xs, ys],
+            dst_ref=raw_in[k].at[...],
+            send_sem=send_sems.at[k],
+            recv_sem=recv_sems.at[k],
+            device_id=(gx + dx, gy + dy),
+            device_id_type=MESH,
+        )
+
+    @pl.when(leads(0, 0))
+    def _():
+        pl.semaphore_wait(barrier, count)
+        for k, (dx, dy) in enumerate(SIDES):
+            if (-dx, -dy) in LOWER:
+                @pl.when(present(dx, dy))
+                def _():
+                    straight(k).start()
+        for dx, dy in LOWER:
+            @pl.when(present(-dx, -dy))
+            def _():
+                pl.semaphore_signal(
+                    ready, inc=1, device_id=(gx - dx, gy - dy), device_id_type=MESH
+                )
+
+    for c in copies_in[1:]:
+        c.start()
+    table_copies = [
+        pltpu.make_async_copy(m2l.at[i], table.at[i], table_sems.at[i]) for i in range(7)
+    ]
+    for c in table_copies:
+        c.start()
+
+    def take(block, y0, x0):
+        block = block.astype(F32)
+        for y in range(block.shape[1]):
+            for x in range(block.shape[0]):
+                tile = jnp.concatenate(
+                    [block[x, y : y + 1, 128 * z : 128 * z + 128] for z in range(8)], axis=0
+                )
+                cells[y0 + y, x0 + x] = tile.astype(BF)
+
+    for dx, dy in SIDES:
+        @pl.when(jnp.logical_not(present(dx, dy)))
+        def _():
+            ys, xs = TARGET[-dy], TARGET[-dx]
+            cells[ys, xs] = jnp.zeros((ys.stop - ys.start, xs.stop - xs.start, 8, 128), BF)
+
+    copies_in[0].wait()
+    take(raw[...], HALO, HALO)
+
+    @pl.when(jnp.logical_not(leads(0, 0)))
+    def _():
+        pl.semaphore_wait(barrier, count)
+
     for k, (dx, dy) in enumerate(SIDES):
-        @pl.when(beside(dx, dy))
+        @pl.when(beside(dx, dy) & jnp.logical_not(leads(0, 0)))
         def _():
             remote(k).start()
 
     def arrive(sides):
         for k, (dx, dy) in enumerate(SIDES):
             if (dx, dy) in sides:
-                @pl.when(present(-dx, -dy))
+                @pl.when(beside(-dx, -dy))
                 def _():
                     remote(k).wait_recv()
+
+                if (-dx, -dy) in LOWER:
+                    @pl.when(leads(-dx, -dy))
+                    def _():
+                        straight(k).wait_recv()
+                        ys, xs = TARGET[dy], TARGET[dx]
+                        take(raw_in[k][...], ys.start, xs.start)
 
     for c in copies_in[1:]:
         c.wait()
@@ -387,9 +422,14 @@
                 out[x, y : y + 1, 128 * z : 128 * z + 128] = value[z : z + 1]
 
     for k, (dx, dy) in enumerate(SIDES):
-        @pl.when(present(dx, dy))
+        @pl.when(present(dx, dy) & jnp.logical_not(leads(0, 0)))
         def _():
             remote(k).wait_send()
+
+        if (-dx, -dy) in LOWER:
+            @pl.when(present(dx, dy) & leads(0, 0))
+            def _():
+                straight(k).wait_send()
 
 
 def local(density, p2m_operator, m2l_table, near_table, l2p_operator):
@@ -424,6 +464,9 @@
             pltpu.VMEM((2, 2, 16, 128), F32),
             pltpu.VMEM((32, 128), F32),
             pltpu.VMEM((32, 128), F32),
+            pltpu.VMEM((2, 2, 1024), BF),
+            pltpu.VMEM((4, 2, 1024), BF),
+            pltpu.VMEM((2, 4, 1024), BF),
             pltpu.SemaphoreType.DMA((4,)),
             pltpu.SemaphoreType.DMA((7,)),
             pltpu.SemaphoreType.DMA((8,)),

time: 18.4 us -> 17.8 us (0.967)
  the two profiles are of different devices: /device:TPU:9 before, /device:TPU:1 now
where the time goes in v6:
time: 17.8 us; the launch traced here: 17.5 us
  Pallas kernels  16.9 us (95%)
  local copies, waits for them, and re-layouts  0.63 us (4%)
    pallas_call x1, Pallas kernels, local(): pl.pallas_call(kernel, out_shape=jax.ShapeDtypeStruct(density.shape, F32)...  16.9 us
    unnamed x1, local copies, waits for them, and re-layouts  0.63 us

profile of v6, /device:TPU:1, one launch (start us, length us, event | category | flops | bytes accessed | tf_op | source)
XLA Modules:
  0.0 17.5 jit_solution(4481373608256428234)
XLA Ops:
  0.0 16.9 %shard_map.55 = f32[4,4,1024]{2,1,0:T(4,128)S(1)} custom-call(bf16[4,4,1024]{2,1,0:T(4,128)(2,1)} %density.1, bf16[56,64]{1,0:T(8,128)(2,1)} %bitcast.1, bf16[7,7,7,56,56]{4,3,2,1,0:T(8,128)(2,1)} %m2l.1, bf16[3,3,3,64,64]{4,3,2,1,0:T(8,128)(2,1)} %near.1, bf16[56,64]{1,0:T(8,128)(2,1)} %l2p.1), custom_call_target="tpu_custom_call" | custom-call | tf_op jit(solution)/shard_map/pallas_call | solution.py:441
  16.9 0.6 %copy.7 = f32[4,4,1024]{2,1,0:T(4,128)} copy(f32[4,4,1024]{2,1,0:T(4,128)S(1)} %shard_map.55) | data formatting | bytes 131072

commit v7 on v6

--- a/solution.py
+++ b/solution.py
@@ -86,7 +86,6 @@
         pltpu.make_async_copy(p2m_t, p2m_raw, in_sems.at[2]),
         pltpu.make_async_copy(l2p, l2p_raw, in_sems.at[3]),
     ]
-    copies_in[0].start()
     barrier = pltpu.get_barrier_semaphore()
 
     def leads(dx, dy):
@@ -95,15 +94,15 @@
     def beside(dx, dy):
         return present(dx, dy) & jnp.logical_not(leads(dx, dy))
 
-    count = jnp.int32(0)
-    for dx, dy in SIDES:
-        count = count + beside(dx, dy).astype(jnp.int32)
-
-        @pl.when(present(dx, dy) & jnp.logical_not(leads(0, 0)))
-        def _():
-            pl.semaphore_signal(
-                barrier, inc=1, device_id=(gx + dx, gy + dy), device_id_type=MESH
-            )
+    @pl.when(jnp.logical_not(leads(0, 0)))
+    def _():
+        for dx, dy in SIDES:
+            @pl.when(present(dx, dy))
+            def _():
+                pl.semaphore_signal(
+                    barrier, inc=1, device_id=(gx + dx, gy + dy), device_id_type=MESH
+                )
+
     def remote(k):
         dx, dy = SIDES[k]
         return pltpu.make_async_remote_copy(
@@ -129,7 +128,9 @@
 
     @pl.when(leads(0, 0))
     def _():
-        pl.semaphore_wait(barrier, count)
+        pl.semaphore_wait(
+            barrier, sum(present(-dx, -dy).astype(jnp.int32) for dx, dy in LOWER)
+        )
         for k, (dx, dy) in enumerate(SIDES):
             if (-dx, -dy) in LOWER:
                 @pl.when(present(dx, dy))
@@ -142,7 +143,7 @@
                     ready, inc=1, device_id=(gx - dx, gy - dy), device_id_type=MESH
                 )
 
-    for c in copies_in[1:]:
+    for c in copies_in:
         c.start()
     table_copies = [
         pltpu.make_async_copy(m2l.at[i], table.at[i], table_sems.at[i]) for i in range(7)
@@ -168,15 +169,6 @@
     copies_in[0].wait()
     take(raw[...], HALO, HALO)
 
-    @pl.when(jnp.logical_not(leads(0, 0)))
-    def _():
-        pl.semaphore_wait(barrier, count)
-
-    for k, (dx, dy) in enumerate(SIDES):
-        @pl.when(beside(dx, dy) & jnp.logical_not(leads(0, 0)))
-        def _():
-            remote(k).start()
-
     def arrive(sides):
         for k, (dx, dy) in enumerate(SIDES):
             if (dx, dy) in sides:
@@ -208,6 +200,17 @@
         return carry
 
     lax.fori_loop(0, 9, build_near, 0, unroll=9)
+
+    @pl.when(jnp.logical_not(leads(0, 0)))
+    def _():
+        pl.semaphore_wait(
+            barrier, sum(beside(dx, dy).astype(jnp.int32) for dx, dy in SIDES)
+        )
+
+    for k, (dx, dy) in enumerate(SIDES):
+        @pl.when(beside(dx, dy) & jnp.logical_not(leads(0, 0)))
+        def _():
+            remote(k).start()
 
     for ox in range(7):
         table_copies[ox].wait()

time: 17.8 us -> 17.7 us (level)
  no operation moved by 1% of the time
where the time goes in v7:
time: 17.7 us; the launch traced here: 17.5 us
  Pallas kernels  16.8 us (95%)
  local copies, waits for them, and re-layouts  0.63 us (4%)
    pallas_call x1, Pallas kernels, local(): pl.pallas_call(kernel, out_shape=jax.ShapeDtypeStruct(density.shape, F32)...  16.8 us
    unnamed x1, local copies, waits for them, and re-layouts  0.63 us

profile of v7, /device:TPU:1, one launch (start us, length us, event | category | flops | bytes accessed | tf_op | source)
XLA Modules:
  0.0 17.5 jit_solution(4070343025253563411)
XLA Ops:
  0.0 16.8 %shard_map.55 = f32[4,4,1024]{2,1,0:T(4,128)S(1)} custom-call(bf16[4,4,1024]{2,1,0:T(4,128)(2,1)} %density.1, bf16[56,64]{1,0:T(8,128)(2,1)} %bitcast.1, bf16[7,7,7,56,56]{4,3,2,1,0:T(8,128)(2,1)} %m2l.1, bf16[3,3,3,64,64]{4,3,2,1,0:T(8,128)(2,1)} %near.1, bf16[56,64]{1,0:T(8,128)(2,1)} %l2p.1), custom_call_target="tpu_custom_call" | custom-call | tf_op jit(solution)/shard_map/pallas_call | solution.py:444
  16.8 0.6 %copy.7 = f32[4,4,1024]{2,1,0:T(4,128)} copy(f32[4,4,1024]{2,1,0:T(4,128)S(1)} %shard_map.55) | data formatting | bytes 131072

commit v8 on v7

--- a/solution.py
+++ b/solution.py
@@ -66,7 +66,7 @@
     raw, cells, table, near_raw, p2m_raw, l2p_raw, weights, near_weights,
     far_rows, near_rows, far_x, far_y, near_x, near_y, total_ref, close_ref,
     far_late_x, far_late_y, near_late_x, near_late_y, raw_corner, raw_y, raw_x,
-    in_sems, table_sems, send_sems, recv_sems, ready,
+    in_sems, send_sems, recv_sems, ready,
 ):
     raw_in = [raw_corner, raw_y, raw_x]
     gx, gy = lax.axis_index("gx"), lax.axis_index("gy")
@@ -145,11 +145,8 @@
 
     for c in copies_in:
         c.start()
-    table_copies = [
-        pltpu.make_async_copy(m2l.at[i], table.at[i], table_sems.at[i]) for i in range(7)
-    ]
-    for c in table_copies:
-        c.start()
+    table_copy = pltpu.make_async_copy(m2l, table, in_sems.at[4])
+    table_copy.start()
 
     def take(block, y0, x0):
         block = block.astype(F32)
@@ -212,9 +209,8 @@
         def _():
             remote(k).start()
 
+    table_copy.wait()
     for ox in range(7):
-        table_copies[ox].wait()
-
         def build(oy, carry):
             blocks = [widen(table[ox, oy, k]) for k in range(7)]
             for k in range(6):
@@ -327,6 +323,15 @@
             place(acc, ys, pars)
 
     for k, (dx, dy) in enumerate(SIDES):
+        @pl.when(beside(dx, dy) & jnp.logical_not(leads(0, 0)))
+        def _():
+            remote(k).wait_send()
+
+        if (-dx, -dy) in LOWER:
+            @pl.when(present(dx, dy) & leads(0, 0))
+            def _():
+                straight(k).wait_send()
+    for k, (dx, dy) in enumerate(SIDES):
         if (dx, dy) in LOWER:
             @pl.when(leads(dx, dy))
             def _():
@@ -339,7 +344,7 @@
         rhs = jnp.concatenate([near_weights[i] for i in places], axis=0)
         near_late[...] = dot(lhs, rhs)
         sums = {}
-        for units, pairs in late_products(axis).items():
+        for units, pairs in sorted(late_products(axis).items(), key=lambda c: -len(c[0])):
             columns = []
             for ox, oy in pairs:
                 across = oy if axis == "x" else ox
@@ -425,14 +430,10 @@
                 out[x, y : y + 1, 128 * z : 128 * z + 128] = value[z : z + 1]
 
     for k, (dx, dy) in enumerate(SIDES):
-        @pl.when(present(dx, dy) & jnp.logical_not(leads(0, 0)))
-        def _():
-            remote(k).wait_send()
-
-        if (-dx, -dy) in LOWER:
-            @pl.when(present(dx, dy) & leads(0, 0))
+        if (dx, dy) in LOWER:
+            @pl.when(leads(dx, dy))
             def _():
-                straight(k).wait_send()
+                remote(k).wait_send()
 
 
 def local(density, p2m_operator, m2l_table, near_table, l2p_operator):
@@ -470,8 +471,7 @@
             pltpu.VMEM((2, 2, 1024), BF),
             pltpu.VMEM((4, 2, 1024), BF),
             pltpu.VMEM((2, 4, 1024), BF),
-            pltpu.SemaphoreType.DMA((4,)),
-            pltpu.SemaphoreType.DMA((7,)),
+            pltpu.SemaphoreType.DMA((5,)),
             pltpu.SemaphoreType.DMA((8,)),
             pltpu.SemaphoreType.DMA((8,)),
             pltpu.SemaphoreType.REGULAR,

time: 17.7 us -> 17.6 us (level)
  no operation moved by 1% of the time
where the time goes in v8:
time: 17.6 us; the launch traced here: 17.4 us
  Pallas kernels  16.7 us (95%)
  local copies, waits for them, and re-layouts  0.63 us (4%)
    pallas_call x1, Pallas kernels, local(): pl.pallas_call(kernel, out_shape=jax.ShapeDtypeStruct(density.shape, F32)...  16.7 us
    unnamed x1, local copies, waits for them, and re-layouts  0.63 us

profile of v8, /device:TPU:1, one launch (start us, length us, event | category | flops | bytes accessed | tf_op | source)
XLA Modules:
  0.0 17.4 jit_solution(15287886951299564770)
XLA Ops:
  0.0 16.7 %shard_map.55 = f32[4,4,1024]{2,1,0:T(4,128)S(1)} custom-call(bf16[4,4,1024]{2,1,0:T(4,128)(2,1)} %density.1, bf16[56,64]{1,0:T(8,128)(2,1)} %bitcast.1, bf16[7,7,7,56,56]{4,3,2,1,0:T(8,128)(2,1)} %m2l.1, bf16[3,3,3,64,64]{4,3,2,1,0:T(8,128)(2,1)} %near.1, bf16[56,64]{1,0:T(8,128)(2,1)} %l2p.1), custom_call_target="tpu_custom_call" | custom-call | tf_op jit(solution)/shard_map/pallas_call | solution.py:445
  16.7 0.6 %copy.7 = f32[4,4,1024]{2,1,0:T(4,128)} copy(f32[4,4,1024]{2,1,0:T(4,128)S(1)} %shard_map.55) | data formatting | bytes 131072

commit v9 on v8

--- a/solution.py
+++ b/solution.py
@@ -9,7 +9,7 @@
 F32 = jnp.float32
 MESH = pl.DeviceIdType.MESH
 HALO = 2
-SIDES = [(1, 1), (0, 1), (1, 0), (1, -1), (-1, 1), (-1, 0), (0, -1), (-1, -1)]
+SIDES = [(0, 1), (1, 1), (1, 0), (1, -1), (-1, 1), (-1, 0), (0, -1), (-1, -1)]
 LOWER = [(-1, 0), (0, -1), (-1, -1)]
 SOURCE = {-1: slice(2, 4), 0: slice(2, 6), 1: slice(4, 6)}
 RAW = {0: slice(0, 4), 1: slice(2, 4)}
@@ -68,7 +68,7 @@
     far_late_x, far_late_y, near_late_x, near_late_y, raw_corner, raw_y, raw_x,
     in_sems, send_sems, recv_sems, ready,
 ):
-    raw_in = [raw_corner, raw_y, raw_x]
+    raw_in = [raw_y, raw_corner, raw_x]
     gx, gy = lax.axis_index("gx"), lax.axis_index("gy")
     nx, ny = lax.axis_size("gx"), lax.axis_size("gy")
 
@@ -426,8 +426,7 @@
                 value = value + eight(near_late_x[...], 2 * (y % 2) + y // 2)
             if y == 0:
                 value = value + eight(near_late_y[...], 2 * (x % 2) + x // 2)
-            for z in range(8):
-                out[x, y : y + 1, 128 * z : 128 * z + 128] = value[z : z + 1]
+            out[x, pl.ds(y, 8, stride=4), :] = value
 
     for k, (dx, dy) in enumerate(SIDES):
         if (dx, dy) in LOWER:
@@ -442,9 +441,9 @@
         pltpu.with_memory_space_constraint(v, pltpu.HBM)
         for v in (density, p2m_operator.T, m2l_table, near_table, l2p_operator)
     ]
-    return pl.pallas_call(
+    rows = pl.pallas_call(
         kernel,
-        out_shape=jax.ShapeDtypeStruct(density.shape, F32),
+        out_shape=jax.ShapeDtypeStruct((4, 32, 128), F32),
         in_specs=[in_hbm] * 5,
         out_specs=pl.BlockSpec(memory_space=pltpu.VMEM),
         scratch_shapes=[
@@ -480,6 +479,7 @@
             collective_id=0, has_side_effects=True, vmem_limit_bytes=32 * 1024 * 1024
         ),
     )(*operands)
+    return rows.reshape(4, 8, 4, 128).transpose(0, 2, 1, 3).reshape(density.shape)
 
 
 def solution(mesh):

time: 17.6 us -> 17.8 us (1.011)
  the two profiles are of different devices: /device:TPU:1 before, /device:TPU:9 now
where the time goes in v9:
time: 17.8 us; the launch traced here: 17.6 us
  Pallas kernels  17 us (96%)
  local copies, waits for them, and re-layouts  0.63 us (4%)
    pallas_call x1, Pallas kernels, local(): pl.pallas_call(kernel, out_shape=jax.ShapeDtypeStruct((4, 32, 128), F32),...  17 us
    unnamed x1, local copies, waits for them, and re-layouts  0.63 us

profile of v9, /device:TPU:9, one launch (start us, length us, event | category | flops | bytes accessed | tf_op | source)
XLA Modules:
  0.0 17.6 jit_solution(9939038108522312298)
XLA Ops:
  0.0 17.0 %shard_map.55 = f32[4,32,128]{2,1,0:T(8,128)S(1)} custom-call(bf16[4,4,1024]{2,1,0:T(4,128)(2,1)} %density.1, bf16[56,64]{1,0:T(8,128)(2,1)} %bitcast.7, bf16[7,7,7,56,56]{4,3,2,1,0:T(8,128)(2,1)} %m2l.1, bf16[3,3,3,64,64]{4,3,2,1,0:T(8,128)(2,1)} %near.1, bf16[56,64]{1,0:T(8,128)(2,1)} %l2p.1), custom_call_target="tpu_custom_call" | custom-call | tf_op jit(solution)/shard_map/pallas_call | solution.py:444
  17.0 0.6 %copy.8 = f32[4,4,1024]{2,1,0:T(4,128)} copy(f32[4,4,1024]{2,1,0:T(4,128)S(1)} %bitcast.6) | data formatting | bytes 131072

commit v10 on v9

--- a/solution.py
+++ b/solution.py
@@ -9,7 +9,7 @@
 F32 = jnp.float32
 MESH = pl.DeviceIdType.MESH
 HALO = 2
-SIDES = [(0, 1), (1, 1), (1, 0), (1, -1), (-1, 1), (-1, 0), (0, -1), (-1, -1)]
+SIDES = [(1, 1), (0, 1), (1, 0), (1, -1), (-1, 1), (-1, 0), (0, -1), (-1, -1)]
 LOWER = [(-1, 0), (0, -1), (-1, -1)]
 SOURCE = {-1: slice(2, 4), 0: slice(2, 6), 1: slice(4, 6)}
 RAW = {0: slice(0, 4), 1: slice(2, 4)}
@@ -68,7 +68,7 @@
     far_late_x, far_late_y, near_late_x, near_late_y, raw_corner, raw_y, raw_x,
     in_sems, send_sems, recv_sems, ready,
 ):
-    raw_in = [raw_y, raw_corner, raw_x]
+    raw_in = [raw_corner, raw_y, raw_x]
     gx, gy = lax.axis_index("gx"), lax.axis_index("gy")
     nx, ny = lax.axis_size("gx"), lax.axis_size("gy")
 
@@ -116,9 +116,8 @@
 
     def straight(k):
         dx, dy = SIDES[k]
-        xs, ys = RAW[dx], RAW[dy]
         return pltpu.make_async_remote_copy(
-            src_ref=density.at[xs, ys],
+            src_ref=density.at[RAW[dx]],
             dst_ref=raw_in[k].at[...],
             send_sem=send_sems.at[k],
             recv_sem=recv_sems.at[k],
@@ -148,14 +147,14 @@
     table_copy = pltpu.make_async_copy(m2l, table, in_sems.at[4])
     table_copy.start()
 
-    def take(block, y0, x0):
+    def take(block, ys, y0, x0):
         block = block.astype(F32)
-        for y in range(block.shape[1]):
+        for i, y in enumerate(range(ys.start, ys.stop)):
             for x in range(block.shape[0]):
                 tile = jnp.concatenate(
                     [block[x, y : y + 1, 128 * z : 128 * z + 128] for z in range(8)], axis=0
                 )
-                cells[y0 + y, x0 + x] = tile.astype(BF)
+                cells[y0 + i, x0 + x] = tile.astype(BF)
 
     for dx, dy in SIDES:
         @pl.when(jnp.logical_not(present(dx, dy)))
@@ -164,7 +163,7 @@
             cells[ys, xs] = jnp.zeros((ys.stop - ys.start, xs.stop - xs.start, 8, 128), BF)
 
     copies_in[0].wait()
-    take(raw[...], HALO, HALO)
+    take(raw[...], slice(0, 4), HALO, HALO)
 
     def arrive(sides):
         for k, (dx, dy) in enumerate(SIDES):
@@ -178,7 +177,7 @@
                     def _():
                         straight(k).wait_recv()
                         ys, xs = TARGET[dy], TARGET[dx]
-                        take(raw_in[k][...], ys.start, xs.start)
+                        take(raw_in[k][...], RAW[dy], ys.start, xs.start)
 
     for c in copies_in[1:]:
         c.wait()
@@ -467,8 +466,8 @@
             pltpu.VMEM((2, 2, 16, 128), F32),
             pltpu.VMEM((32, 128), F32),
             pltpu.VMEM((32, 128), F32),
-            pltpu.VMEM((2, 2, 1024), BF),
-            pltpu.VMEM((4, 2, 1024), BF),
+            pltpu.VMEM((2, 4, 1024), BF),
+            pltpu.VMEM((4, 4, 1024), BF),
             pltpu.VMEM((2, 4, 1024), BF),
             pltpu.SemaphoreType.DMA((5,)),
             pltpu.SemaphoreType.DMA((8,)),

time: 17.8 us -> 17.8 us (level)
  the two profiles are of different devices: /device:TPU:9 before, /device:TPU:8 now
where the time goes in v10:
time: 17.8 us; the launch traced here: 17.7 us
  Pallas kernels  17.1 us (96%)
  local copies, waits for them, and re-layouts  0.63 us (4%)
    pallas_call x1, Pallas kernels, local(): pl.pallas_call(kernel, out_shape=jax.ShapeDtypeStruct((4, 32, 128), F32),...  17.1 us
    unnamed x1, local copies, waits for them, and re-layouts  0.63 us

profile of v10, /device:TPU:8, one launch (start us, length us, event | category | flops | bytes accessed | tf_op | source)
XLA Modules:
  0.0 17.7 jit_solution(16537365204724835570)
XLA Ops:
  0.0 17.1 %shard_map.55 = f32[4,32,128]{2,1,0:T(8,128)S(1)} custom-call(bf16[4,4,1024]{2,1,0:T(4,128)(2,1)} %density.1, bf16[56,64]{1,0:T(8,128)(2,1)} %bitcast.7, bf16[7,7,7,56,56]{4,3,2,1,0:T(8,128)(2,1)} %m2l.1, bf16[3,3,3,64,64]{4,3,2,1,0:T(8,128)(2,1)} %near.1, bf16[56,64]{1,0:T(8,128)(2,1)} %l2p.1), custom_call_target="tpu_custom_call" | custom-call | tf_op jit(solution)/shard_map/pallas_call | solution.py:443
  17.1 0.6 %copy.8 = f32[4,4,1024]{2,1,0:T(4,128)} copy(f32[4,4,1024]{2,1,0:T(4,128)S(1)} %bitcast.6) | data formatting | bytes 131072

commit v11 on v9

--- a/solution.py
+++ b/solution.py
@@ -9,7 +9,7 @@
 F32 = jnp.float32
 MESH = pl.DeviceIdType.MESH
 HALO = 2
-SIDES = [(0, 1), (1, 1), (1, 0), (1, -1), (-1, 1), (-1, 0), (0, -1), (-1, -1)]
+SIDES = [(1, 1), (0, 1), (1, 0), (1, -1), (-1, 1), (-1, 0), (0, -1), (-1, -1)]
 LOWER = [(-1, 0), (0, -1), (-1, -1)]
 SOURCE = {-1: slice(2, 4), 0: slice(2, 6), 1: slice(4, 6)}
 RAW = {0: slice(0, 4), 1: slice(2, 4)}
@@ -68,7 +68,7 @@
     far_late_x, far_late_y, near_late_x, near_late_y, raw_corner, raw_y, raw_x,
     in_sems, send_sems, recv_sems, ready,
 ):
-    raw_in = [raw_y, raw_corner, raw_x]
+    raw_in = [raw_corner, raw_y, raw_x]
     gx, gy = lax.axis_index("gx"), lax.axis_index("gy")
     nx, ny = lax.axis_size("gx"), lax.axis_size("gy")
 

time: 17.8 us -> 17.6 us (0.989)
  the two profiles are of different devices: /device:TPU:9 before, /device:TPU:1 now
where the time goes in v11:
time: 17.6 us; the launch traced here: 17.4 us
  Pallas kernels  16.7 us (95%)
  local copies, waits for them, and re-layouts  0.63 us (4%)
    pallas_call x1, Pallas kernels, local(): pl.pallas_call(kernel, out_shape=jax.ShapeDtypeStruct((4, 32, 128), F32),...  16.7 us
    unnamed x1, local copies, waits for them, and re-layouts  0.63 us

profile of v11, /device:TPU:1, one launch (start us, length us, event | category | flops | bytes accessed | tf_op | source)
XLA Modules:
  0.0 17.4 jit_solution(14538329403444910586)
XLA Ops:
  0.0 16.7 %shard_map.55 = f32[4,32,128]{2,1,0:T(8,128)S(1)} custom-call(bf16[4,4,1024]{2,1,0:T(4,128)(2,1)} %density.1, bf16[56,64]{1,0:T(8,128)(2,1)} %bitcast.7, bf16[7,7,7,56,56]{4,3,2,1,0:T(8,128)(2,1)} %m2l.1, bf16[3,3,3,64,64]{4,3,2,1,0:T(8,128)(2,1)} %near.1, bf16[56,64]{1,0:T(8,128)(2,1)} %l2p.1), custom_call_target="tpu_custom_call" | custom-call | tf_op jit(solution)/shard_map/pallas_call | solution.py:444
  16.7 0.6 %copy.8 = f32[4,4,1024]{2,1,0:T(4,128)} copy(f32[4,4,1024]{2,1,0:T(4,128)S(1)} %bitcast.6) | data formatting | bytes 131072

commit v12 on v8

--- a/solution.py
+++ b/solution.py
@@ -362,12 +362,17 @@
         for t, p in sums:
             far_late[t, p] = sums[t, p]
 
-    arrive([side for side in SIDES if side in ((0, 1), (-1, 1))])
+    @pl.when(gx == 0)
+    def _():
+        far_late_x[...] = jnp.zeros_like(far_late_x)
+        near_late_x[...] = jnp.zeros_like(near_late_x)
 
     @pl.when(gy == 0)
     def _():
         far_late_y[...] = jnp.zeros_like(far_late_y)
         near_late_y[...] = jnp.zeros_like(near_late_y)
+
+    arrive([side for side in SIDES if side in ((0, 1), (-1, 1))])
 
     @pl.when(gy > 0)
     def _():
@@ -386,11 +391,6 @@
         late("y", far_y, near_y, far_late_y, near_late_y)
 
     arrive([side for side in SIDES if side in ((1, 0), (1, 1), (1, -1))])
-
-    @pl.when(gx == 0)
-    def _():
-        far_late_x[...] = jnp.zeros_like(far_late_x)
-        near_late_x[...] = jnp.zeros_like(near_late_x)
 
     @pl.when(gx > 0)
     def _():

time: 17.6 us -> 17.6 us (level)
  no operation moved by 1% of the time
where the time goes in v12:
time: 17.6 us; the launch traced here: 17.4 us
  Pallas kernels  16.7 us (95%)
  local copies, waits for them, and re-layouts  0.63 us (4%)
    pallas_call x1, Pallas kernels, local(): pl.pallas_call(kernel, out_shape=jax.ShapeDtypeStruct(density.shape, F32)...  16.7 us
    unnamed x1, local copies, waits for them, and re-layouts  0.63 us

profile of v12, /device:TPU:1, one launch (start us, length us, event | category | flops | bytes accessed | tf_op | source)
XLA Modules:
  0.0 17.4 jit_solution(3106495166186402629)
XLA Ops:
  0.0 16.7 %shard_map.55 = f32[4,4,1024]{2,1,0:T(4,128)S(1)} custom-call(bf16[4,4,1024]{2,1,0:T(4,128)(2,1)} %density.1, bf16[56,64]{1,0:T(8,128)(2,1)} %bitcast.1, bf16[7,7,7,56,56]{4,3,2,1,0:T(8,128)(2,1)} %m2l.1, bf16[3,3,3,64,64]{4,3,2,1,0:T(8,128)(2,1)} %near.1, bf16[56,64]{1,0:T(8,128)(2,1)} %l2p.1), custom_call_target="tpu_custom_call" | custom-call | tf_op jit(solution)/shard_map/pallas_call | solution.py:445
  16.7 0.6 %copy.7 = f32[4,4,1024]{2,1,0:T(4,128)} copy(f32[4,4,1024]{2,1,0:T(4,128)S(1)} %shard_map.55) | data formatting | bytes 131072
